TPU v7x, 32 devices: a whole 2x2x4 slice. The times are simulated.
32 devices in a mesh: group: 8 (over z, x), shard: 4 (over y, core).
Axes of the slice: x: 2, y: 2, z: 4, core: 2. Of those that a mesh axis runs over, the one named last changes fastest.
Arguments:
- inputs: bfloat16 [2, 8, 1024, 768], P(None, 'group', 'shard'), may hold values from -6 to 6
- block_ids: int32 [2, 8, 1024], P(None, 'group'), may hold values from 0 to 7, never falling along the last dimension, each value on 1 to 256 neighbouring positions
- attn_gain: bfloat16 [768], P('shard'), may hold values from 0.099609375 to 1.8984375
- attn_shift: bfloat16 [768], P('shard'), may hold values from -2 to 2
- weight_qkv: bfloat16 [768, 2304], P('shard'), may hold values from -0.3125 to 0.3125
- bias_qv: bfloat16 [1536], P('shard'), may hold values from -2 to 2
- weight_out: bfloat16 [768, 768], P('shard'), may hold values from -3.5 to 3.5
- bias_out: bfloat16 [768], P('shard'), may hold values from -5 to 5
- mlp_gain: bfloat16 [768], P('shard'), may hold values from 0.099609375 to 1.8984375
- mlp_shift: bfloat16 [768], P('shard'), may hold values from -2 to 2
- weight_up: bfloat16 [768, 3072], P('shard'), may hold values from -0.21875 to 0.21875
- bias_up: bfloat16 [3072], P('shard'), may hold values from -2 to 2
- weight_down: bfloat16 [3072, 768], P('shard'), may hold values from -0.75 to 0.75
- bias_down: bfloat16 [768], P('shard'), may hold values from -5 to 5
- cotangent: bfloat16 [2, 8, 1024, 768], P(None, 'group', 'shard'), may hold values from -6 to 6
Outputs:
- outputs: bfloat16 [2, 8, 1024, 768], P(None, 'group', 'shard')
- grad_inputs: float32 [2, 8, 1024, 768], P(None, 'group', 'shard')
- grad_attn_gain: float32 [768], P('shard')
- grad_attn_shift: float32 [768], P('shard')
- grad_weight_qkv: float32 [768, 2304], P('shard')
- grad_bias_qv: float32 [1536], P('shard')
- grad_weight_out: float32 [768, 768], P('shard')
- grad_bias_out: float32 [768], P('shard')
- grad_mlp_gain: float32 [768], P('shard')
- grad_mlp_shift: float32 [768], P('shard')
- grad_weight_up: float32 [768, 3072], P('shard')
- grad_bias_up: float32 [3072], P('shard')
- grad_weight_down: float32 [3072, 768], P('shard')
- grad_bias_down: float32 [768], P('shard')
Inputs may be any that keep to these rules, and one draw needn't show every extreme that they name: `block_ids`: along each sequence the block ids never fall; each id holds 1 to 256 consecutive positions.
All inputs are finite; a program needn't handle non-finite values.
Results may differ from a plain program's by a relative error of at most 0.017.
The roundings to bfloat16 on the way count: a program that leaves them out, or rounds other values in their place, can miss the bound.
Values may be sent and summed in bfloat16 or wider, within the bound.
No kernel may reach another device: no remote copies, remote signals or barrier semaphores. Data moves between devices by JAX's collectives and lax.ppermute only.
A program may use at most 192 MiB of HBM per device.

v0:
```python
import math

import jax
import jax.numpy as jnp
from jax import lax
from jax.sharding import PartitionSpec as P

HEADS = 12
DEPTH = 48


def norm_rows(rows_in, gain_in, shift_in):
    center = jnp.mean(rows_in, axis=-1, keepdims=True)
    deviate = rows_in - center
    spread = jnp.mean(deviate * deviate, axis=-1, keepdims=True)
    return deviate * lax.rsqrt(spread + 1e-05) * gain_in + shift_in


def gelu_tanh(rows_in):
    return (
        0.5
        * rows_in
        * (1.0 + jnp.tanh(0.7978845608028654 * (rows_in + 0.044715 * rows_in * rows_in * rows_in)))
    )


def masked_scores(query_half, key_half, allowed, scaling):
    scores = (
        jnp.einsum("sqhc,skhc->shqk", query_half, key_half, preferred_element_type=jnp.float32)
        * scaling
    )
    return jnp.where(allowed[:, None, :, :], scores, -1e30)


def attend_half(query_half, key_half, value_half, allowed, scaling):
    scores = masked_scores(query_half, key_half, allowed, scaling)
    top_score = jnp.max(scores, axis=-1, keepdims=True)
    shifted = jnp.exp(scores - top_score)
    totals = jnp.sum(shifted, axis=-1, keepdims=True)
    prob_rows = (shifted / totals).astype(jnp.bfloat16)
    result = jnp.einsum(
        "shqk,skhc->sqhc", prob_rows, value_half, preferred_element_type=jnp.float32
    )
    return (result, top_score + jnp.log(totals))


def attend_back(query_half, key_half, value_half, grad_half, allowed, log_total, scaling):
    scores = masked_scores(query_half, key_half, allowed, scaling)
    prob_rows = jnp.exp(scores - log_total)
    prob_low = prob_rows.astype(jnp.bfloat16)
    grad_value = jnp.einsum(
        "shqk,sqhc->skhc", prob_low, grad_half, preferred_element_type=jnp.float32
    )
    grad_prob = jnp.einsum(
        "sqhc,skhc->shqk", grad_half, value_half, preferred_element_type=jnp.float32
    )
    inner_sum = jnp.sum(prob_rows * grad_prob, axis=-1, keepdims=True)
    grad_scores = (prob_rows * (grad_prob - inner_sum)).astype(jnp.bfloat16)
    grad_query = (
        jnp.einsum("shqk,skhc->sqhc", grad_scores, key_half, preferred_element_type=jnp.float32)
        * scaling
    )
    grad_key = (
        jnp.einsum("shqk,sqhc->skhc", grad_scores, query_half, preferred_element_type=jnp.float32)
        * scaling
    )
    return (grad_query, grad_key, grad_value)


def layer_pass(gathered, inputs_now, ids_now, cot_now, position):
    (
        gain_one,
        shift_one,
        mixing_weight,
        bias_pair,
        attention_weight,
        attention_bias,
        gain_two,
        shift_two,
        inner_layer_weight,
        inner_layer_bias,
        closing_weight,
        closing_bias,
    ) = gathered
    seq_count, block_rows, features = inputs_now.shape
    seq_length = ids_now.shape[1]
    head_width = features // HEADS
    half_heads = HEADS // 2
    half_columns = half_heads * head_width
    scaling = 1.0 / math.sqrt(head_width)
    branch = 1.0 / math.sqrt(DEPTH)
    row_total = seq_count * block_rows
    gain_one_f = gain_one.astype(jnp.float32)
    shift_one_f = shift_one.astype(jnp.float32)
    gain_two_f = gain_two.astype(jnp.float32)
    shift_two_f = shift_two.astype(jnp.float32)
    pair_f = bias_pair.astype(jnp.float32)
    complete_bias = jnp.concatenate(
        [pair_f[:features], jnp.zeros((features,), jnp.float32), pair_f[features:]]
    )
    tokens = inputs_now.astype(jnp.float32).reshape(row_total, features)
    opening_input = norm_rows(tokens, gain_one_f, shift_one_f).astype(jnp.bfloat16)
    query_key_value_mixed = (
        jnp.dot(opening_input, mixing_weight, preferred_element_type=jnp.float32) + complete_bias
    )
    query_rows = (
        query_key_value_mixed[:, :features]
        .astype(jnp.bfloat16)
        .reshape(seq_count, block_rows, features)
    )
    key_rows = (
        query_key_value_mixed[:, features : 2 * features]
        .astype(jnp.bfloat16)
        .reshape(seq_count, block_rows, features)
    )
    value_rows = (
        query_key_value_mixed[:, 2 * features :]
        .astype(jnp.bfloat16)
        .reshape(seq_count, block_rows, features)
    )
    key_all, value_all = (
        lax.all_gather(key_rows, "shard", axis=1, tiled=True),
        lax.all_gather(value_rows, "shard", axis=1, tiled=True),
    )
    query_ids = lax.dynamic_slice_in_dim(ids_now, position, block_rows, 1)
    allowed = ids_now[:, None, :] <= query_ids[:, :, None]

    def heads_of(source, rows_count, start_col):
        return source[:, :, start_col : start_col + half_columns].reshape(
            seq_count, rows_count, half_heads, head_width
        )

    outs_half = []
    totals_half = []
    for half_index in range(2):
        start_col = half_index * half_columns
        result, log_total = attend_half(
            heads_of(query_rows, block_rows, start_col),
            heads_of(key_all, seq_length, start_col),
            heads_of(value_all, seq_length, start_col),
            allowed,
            scaling,
        )
        outs_half.append(result.reshape(seq_count, block_rows, half_columns))
        totals_half.append(log_total)
    attention_mixed = (
        jnp.concatenate(outs_half, axis=2).reshape(row_total, features).astype(jnp.bfloat16)
    )
    attention_output = jnp.dot(
        attention_mixed, attention_weight, preferred_element_type=jnp.float32
    ) + attention_bias.astype(jnp.float32)
    residual = tokens + branch * attention_output
    second_output = norm_rows(residual, gain_two_f, shift_two_f).astype(jnp.bfloat16)
    preactivation = jnp.dot(
        second_output, inner_layer_weight, preferred_element_type=jnp.float32
    ) + inner_layer_bias.astype(jnp.float32)
    hidden_units = gelu_tanh(preactivation).astype(jnp.bfloat16)
    closing_output = jnp.dot(
        hidden_units, closing_weight, preferred_element_type=jnp.float32
    ) + closing_bias.astype(jnp.float32)
    result_rows = (
        (residual + branch * closing_output)
        .astype(jnp.bfloat16)
        .reshape(seq_count, block_rows, features)
    )
    grad_out = cot_now.astype(jnp.float32).reshape(row_total, features)
    grad_final = (branch * grad_out).astype(jnp.bfloat16)
    grad_wfinal = jnp.einsum(
        "rf,rd->fd", hidden_units, grad_final, preferred_element_type=jnp.float32
    )
    grad_bfinal = jnp.sum(grad_final.astype(jnp.float32), axis=0)
    grad_hidden = jnp.einsum(
        "rd,fd->rf", grad_final, closing_weight, preferred_element_type=jnp.float32
    )
    _, gelu_pull = jax.vjp(gelu_tanh, preactivation)
    grad_pre = gelu_pull(grad_hidden)[0].astype(jnp.bfloat16)
    grad_whidden = jnp.einsum(
        "rd,rf->df", second_output, grad_pre, preferred_element_type=jnp.float32
    )
    grad_bhidden = jnp.sum(grad_pre.astype(jnp.float32), axis=0)
    grad_second = jnp.einsum(
        "rf,df->rd", grad_pre, inner_layer_weight, preferred_element_type=jnp.float32
    )
    _, norm_pull = jax.vjp(norm_rows, residual, gain_two_f, shift_two_f)
    grad_resid_part, grad_gain_two, grad_shift_two = norm_pull(grad_second)
    grad_residual = grad_out + grad_resid_part
    grad_attn = (branch * grad_residual).astype(jnp.bfloat16)
    grad_wattn = jnp.einsum(
        "rd,re->de", attention_mixed, grad_attn, preferred_element_type=jnp.float32
    )
    grad_battn = jnp.sum(grad_attn.astype(jnp.float32), axis=0)
    grad_attended = jnp.einsum(
        "re,de->rd", grad_attn, attention_weight, preferred_element_type=jnp.float32
    )
    grad_attended = grad_attended.astype(jnp.bfloat16).reshape(seq_count, block_rows, features)
    query_grads = []
    key_grads = []
    value_grads = []
    for half_index in range(2):
        start_col = half_index * half_columns
        grad_query_h, grad_key_h, grad_value_h = attend_back(
            heads_of(query_rows, block_rows, start_col),
            heads_of(key_all, seq_length, start_col),
            heads_of(value_all, seq_length, start_col),
            heads_of(grad_attended, block_rows, start_col),
            allowed,
            totals_half[half_index],
            scaling,
        )
        query_grads.append(grad_query_h.reshape(seq_count, block_rows, half_columns))
        key_grads.append(grad_key_h.reshape(seq_count, seq_length, half_columns))
        value_grads.append(grad_value_h.reshape(seq_count, seq_length, half_columns))
    grad_query = jnp.concatenate(query_grads, axis=2).astype(jnp.bfloat16)
    key_terms = jnp.concatenate(key_grads, axis=2)
    value_terms = jnp.concatenate(value_grads, axis=2)
    grad_key, grad_value = (
        lax.psum_scatter(key_terms, "shard", scatter_dimension=1, tiled=True),
        lax.psum_scatter(value_terms, "shard", scatter_dimension=1, tiled=True),
    )
    grad_key_low = grad_key.astype(jnp.bfloat16)
    grad_value_low = grad_value.astype(jnp.bfloat16)
    grad_mixed = jnp.concatenate([grad_query, grad_key_low, grad_value_low], axis=2).reshape(
        row_total, 3 * features
    )
    grad_wmix = jnp.einsum(
        "rd,re->de", opening_input, grad_mixed, preferred_element_type=jnp.float32
    )
    mixed_sums = jnp.sum(grad_mixed.astype(jnp.float32), axis=0)
    grad_bpair = jnp.concatenate([mixed_sums[:features], mixed_sums[2 * features :]])
    grad_first = jnp.einsum(
        "re,de->rd", grad_mixed, mixing_weight, preferred_element_type=jnp.float32
    )
    _, first_pull = jax.vjp(norm_rows, tokens, gain_one_f, shift_one_f)
    grad_tok_part, grad_gain_one, grad_shift_one = first_pull(grad_first)
    grad_inputs = (grad_residual + grad_tok_part).reshape(seq_count, block_rows, features)
    grads = (
        grad_gain_one,
        grad_shift_one,
        grad_wmix,
        grad_bpair,
        grad_wattn,
        grad_battn,
        grad_gain_two,
        grad_shift_two,
        grad_whidden,
        grad_bhidden,
        grad_wfinal,
        grad_bfinal,
    )
    return (grads, result_rows, grad_inputs)


def body(
    inputs,
    block_ids,
    attn_gain,
    attn_shift,
    weight_qkv,
    bias_qv,
    weight_out,
    bias_out,
    mlp_gain,
    mlp_shift,
    weight_up,
    bias_up,
    weight_down,
    bias_down,
    cotangent,
):
    micro_count, seq_count, block_rows, features = inputs.shape
    seq_length = block_ids.shape[2]
    position = lax.axis_index("shard") * block_rows
    tokens_all = micro_count * seq_count * seq_length * lax.axis_size("group")
    grad_factor = 1.0 / math.sqrt(tokens_all)
    result_list = []
    grad_list = []
    summed = None
    for micro_index in range(micro_count):
        gathered = (
            lax.all_gather(attn_gain, "shard", axis=0, tiled=True),
            lax.all_gather(attn_shift, "shard", axis=0, tiled=True),
            lax.all_gather(weight_qkv, "shard", axis=0, tiled=True),
            lax.all_gather(bias_qv, "shard", axis=0, tiled=True),
            lax.all_gather(weight_out, "shard", axis=0, tiled=True),
            lax.all_gather(bias_out, "shard", axis=0, tiled=True),
            lax.all_gather(mlp_gain, "shard", axis=0, tiled=True),
            lax.all_gather(mlp_shift, "shard", axis=0, tiled=True),
            lax.all_gather(weight_up, "shard", axis=0, tiled=True),
            lax.all_gather(bias_up, "shard", axis=0, tiled=True),
            lax.all_gather(weight_down, "shard", axis=0, tiled=True),
            lax.all_gather(bias_down, "shard", axis=0, tiled=True),
        )
        partial_value, result_rows, grad_rows = layer_pass(
            gathered, inputs[micro_index], block_ids[micro_index], cotangent[micro_index], position
        )
        result_list.append(result_rows)
        grad_list.append(grad_rows)
        summed = partial_value if micro_index == 0 else jax.tree.map(jnp.add, summed, partial_value)
    (
        full_ga,
        full_sa,
        full_wq,
        full_bq,
        full_wo,
        full_bo,
        full_gm,
        full_sm,
        full_wu,
        full_bu,
        full_wd,
        full_bd,
    ) = summed
    summed = (
        lax.psum_scatter(
            full_ga.astype(jnp.bfloat16), "shard", scatter_dimension=0, tiled=True
        ).astype(jnp.float32),
        lax.psum_scatter(
            full_sa.astype(jnp.bfloat16), "shard", scatter_dimension=0, tiled=True
        ).astype(jnp.float32),
        lax.psum_scatter(
            full_wq.astype(jnp.bfloat16), "shard", scatter_dimension=0, tiled=True
        ).astype(jnp.float32),
        lax.psum_scatter(
            full_bq.astype(jnp.bfloat16), "shard", scatter_dimension=0, tiled=True
        ).astype(jnp.float32),
        lax.psum_scatter(
            full_wo.astype(jnp.bfloat16), "shard", scatter_dimension=0, tiled=True
        ).astype(jnp.float32),
        lax.psum_scatter(
            full_bo.astype(jnp.bfloat16), "shard", scatter_dimension=0, tiled=True
        ).astype(jnp.float32),
        lax.psum_scatter(
            full_gm.astype(jnp.bfloat16), "shard", scatter_dimension=0, tiled=True
        ).astype(jnp.float32),
        lax.psum_scatter(
            full_sm.astype(jnp.bfloat16), "shard", scatter_dimension=0, tiled=True
        ).astype(jnp.float32),
        lax.psum_scatter(
            full_wu.astype(jnp.bfloat16), "shard", scatter_dimension=0, tiled=True
        ).astype(jnp.float32),
        lax.psum_scatter(
            full_bu.astype(jnp.bfloat16), "shard", scatter_dimension=0, tiled=True
        ).astype(jnp.float32),
        lax.psum_scatter(
            full_wd.astype(jnp.bfloat16), "shard", scatter_dimension=0, tiled=True
        ).astype(jnp.float32),
        lax.psum_scatter(
            full_bd.astype(jnp.bfloat16), "shard", scatter_dimension=0, tiled=True
        ).astype(jnp.float32),
    )
    (
        own_ga,
        own_sa,
        own_wq,
        own_bq,
        own_wo,
        own_bo,
        own_gm,
        own_sm,
        own_wu,
        own_bu,
        own_wd,
        own_bd,
    ) = summed
    totals = lax.psum(
        (
            own_ga,
            own_sa,
            own_wq,
            own_bq,
            own_wo,
            own_bo,
            own_gm,
            own_sm,
            own_wu,
            own_bu,
            own_wd,
            own_bd,
        ),
        "group",
    )
    scaled = [member * grad_factor for member in totals]
    return (
        jnp.stack(result_list, axis=0),
        jnp.stack(grad_list, axis=0),
        scaled[0],
        scaled[1],
        scaled[2],
        scaled[3],
        scaled[4],
        scaled[5],
        scaled[6],
        scaled[7],
        scaled[8],
        scaled[9],
        scaled[10],
        scaled[11],
    )


def solution(mesh):
    in_specs = (
        P(None, "group", "shard", None),
        P(None, "group", None),
        P("shard"),
        P("shard"),
        P("shard", None),
        P("shard"),
        P("shard", None),
        P("shard"),
        P("shard"),
        P("shard"),
        P("shard", None),
        P("shard"),
        P("shard", None),
        P("shard"),
        P(None, "group", "shard", None),
    )
    out_specs = (
        P(None, "group", "shard", None),
        P(None, "group", "shard", None),
        P("shard"),
        P("shard"),
        P("shard", None),
        P("shard"),
        P("shard", None),
        P("shard"),
        P("shard"),
        P("shard"),
        P("shard", None),
        P("shard"),
        P("shard", None),
        P("shard"),
    )
    return jax.shard_map(body, mesh=mesh, in_specs=in_specs, out_specs=out_specs, check_vma=False)
```

profile of v0, /device:TPU:0, one launch (start us, length us, event | category | flops | bytes accessed | tf_op | source)
XLA Modules:
  0.0 887.4 jit_solution(188996022816823651)
XLA Ops:
  14.9 13.5 %all-reduce.16 = (bf16[768]{0:T(1024)(128)(2,1)S(1)}, bf16[768]{0:T(1024)(128)(2,1)S(1)}, bf16[768]{0:T(1024)(128)(2,1)S(1)}, bf16[768]{0:T(1024)(128)(2,1)S(1)}, bf16[768]{0:T(1024)(128)(2,1)S(1)}) all-reduce(bf16[768]{0:T(1024)(128)(2,1)S(1)} %dynamic-update-slice.2, ...), channel_id=1, replica_groups=mesh['group'=8,'shard'=4] {'shard'}, use_global_device_ids=true, to_apply=%add.2 | all-reduce | flops 3840 | bytes 15360
  28.4 5.3 all-gather.4
  36.7 6.5 all-gather.15.cloned.1.call-done
  55.4 5.9 all-gather.5
  69.3 20.0 %all-gather.27.cloned.1.call-done = bf16[1024,768]{1,0:T(8,128)(2,1)} async-done(((bf16[256,768]{1,0:T(8,128)(2,1)}), bf16[1024,768]{1,0:T(8,128)(2,1)}) %all-gather.27.cloned.1.call-update) | async-done | bytes 1572880 | tf_op jit(solution)/shard_map/all_gather | solution.py:123
  95.4 15.5 %all-gather.25.cloned.1.call-done = bf16[1024,768]{1,0:T(8,128)(2,1)} async-done(((bf16[256,768]{1,0:T(8,128)(2,1)}), bf16[1024,768]{1,0:T(8,128)(2,1)}) %all-gather.25.cloned.1.call-update) | async-done | bytes 1572880 | tf_op jit(solution)/shard_map/all_gather | solution.py:122
  115.0 17.6 %all-gather.23.cloned.1.call-done = bf16[1024,768]{1,0:T(8,128)(2,1)} async-done(((bf16[256,768]{1,0:T(8,128)(2,1)}), bf16[1024,768]{1,0:T(8,128)(2,1)}) %all-gather.23.cloned.1.call-update) | async-done | bytes 1572880 | tf_op jit(solution)/shard_map/all_gather | solution.py:123
  169.7 20.8 %all-gather.19.cloned.1.call-done = bf16[768,3072]{1,0:T(8,128)(2,1)} async-done(((bf16[192,3072]{1,0:T(8,128)(2,1)}), bf16[768,3072]{1,0:T(8,128)(2,1)}) %all-gather.19.cloned.1.call-update) | async-done | bytes 4718608 | tf_op jit(solution)/shard_map/all_gather | solution.py:288
  190.4 5.6 convolution_add_fusion.3
  196.0 33.4 %all-gather.21.cloned.1.call-done = bf16[3072,768]{1,0:T(8,128)(2,1)} async-done(((bf16[768,768]{1,0:T(8,128)(2,1)}), bf16[3072,768]{1,0:T(8,128)(2,1)}) %all-gather.21.cloned.1.call-update) | async-done | bytes 4718608 | tf_op jit(solution)/shard_map/all_gather | solution.py:290
  229.5 8.3 convert_reduce_fusion.1
  241.9 4.3 convert_reduce_fusion
  252.3 4.1 fusion.26
  264.6 4.8 fusion.22
  274.5 3.9 multiply_reduce_fusion.3
  278.5 3.7 multiply_convert_fusion.3
  291.8 4.4 multiply_reduce_fusion.1
  296.2 3.8 multiply_convert_fusion.1
  312.8 4.4 fusion.122
  317.2 4.0 add_convert_fusion
  325.3 3.8 add_convert_fusion.1
  332.3 4.1 fusion.54
  342.3 35.9 %reduce-scatter.9.cloned.1.call-done = f32[1,256,768]{1,2,0:T(8,128)} async-done(((f32[1,1024,768]{1,2,0:T(8,128)}), f32[1,256,768]{1,2,0:T(8,128)}) %reduce-scatter.9.cloned.1.call-update) | async-done | bytes 786448 | tf_op jit(solution)/shard_map/reduce_scatter | solution.py:217
  379.4 39.0 %reduce-scatter.13.cloned.1.call-done = f32[1,256,768]{1,2,0:T(8,128)} async-done(((f32[1,1024,768]{1,2,0:T(8,128)}), f32[1,256,768]{1,2,0:T(8,128)}) %reduce-scatter.13.cloned.1.call-update) | async-done | bytes 786448 | tf_op jit(solution)/shard_map/reduce_scatter | solution.py:217
  427.1 20.0 %reduce-scatter.19.cloned.1.call-done = bf16[192,768]{1,0:T(8,128)(2,1)} async-done(((bf16[768,768]{1,0:T(8,128)(2,1)}), bf16[192,768]{1,0:T(8,128)(2,1)}) %reduce-scatter.19.cloned.1.call-update) | async-done | bytes 294928 | tf_op jit(solution)/shard_map/reduce_scatter | solution.py:326
  455.1 11.2 %all-reduce.15 = (bf16[768]{0:T(1024)(128)(2,1)S(1)}, bf16[768]{0:T(1024)(128)(2,1)S(1)}, bf16[768]{0:T(1024)(128)(2,1)S(1)}, bf16[1536]{0:T(1024)(128)(2,1)S(1)...) all-reduce(bf16[768]{0:T(1024)(128)(2,1)} %copy-done.130, ...), channel_id=1, replica_groups=mesh['group'=8,'shard'=4] {'shard'}, use_global_device_ids=true, to_apply=%add.5 | all-reduce | flops 9984 | bytes 39936
  466.9 6.2 fusion.50
  473.1 4.5 fusion.51
  480.6 16.9 %reduce-scatter.23.cloned.1.call-done = bf16[768,768]{1,0:T(8,128)(2,1)} async-done(((bf16[3072,768]{1,0:T(8,128)(2,1)}), bf16[768,768]{1,0:T(8,128)(2,1)}) %reduce-scatter.23.cloned.1.call-update) | async-done | bytes 1179664 | tf_op jit(solution)/shard_map/reduce_scatter | solution.py:344
  497.5 50.4 %reduce-scatter.21.cloned.1.call-done = bf16[192,3072]{1,0:T(8,128)(2,1)} async-done(((bf16[768,3072]{1,0:T(8,128)(2,1)}), bf16[192,3072]{1,0:T(8,128)(2,1)}) %reduce-scatter.21.cloned.1.call-update) | async-done | bytes 1179664 | tf_op jit(solution)/shard_map/reduce_scatter | solution.py:338
  547.9 42.8 %reduce-scatter.17.cloned.1.call-done = bf16[192,2304]{1,0:T(8,128)(2,1)} async-done(((bf16[768,2304]{1,0:T(8,128)(2,1)}), bf16[192,2304]{1,0:T(8,128)(2,1)}) %reduce-scatter.17.cloned.1.call-update) | async-done | bytes 884752 | tf_op jit(solution)/shard_map/reduce_scatter | solution.py:320
  590.7 278.6 %all-reduce.18 = (f32[192]{0:T(256)S(1)}, f32[192]{0:T(256)S(1)}, f32[192,2304]{1,0:T(8,128)}, f32[384]{0:T(512)S(1)}, f32[192,768]{1,0:T(8,128)S(1)}, /*index=5...) all-reduce(f32[192]{0:T(256)S(1)} %dynamic-slice_convert_fusion.7, ...), channel_id=1, replica_groups=mesh['group'=8,'shard'=4] {'group'}, use_global_device_ids=true, to_apply=%region_35.36 | all-reduce | flops 1771776 | bytes 10635264 | tf_op jit(solution)/shard_map/psum | solution.py:365
  (509 shorter events, 165.4 us)
Async XLA Ops:
  7.2 36.1 %all-gather.15.cloned.1.call-start = ((), (), s32[]{:S(2)}) async-start(), calls=%async_computation.8 | async-start | bytes 4423680 | tf_op jit(solution)/shard_map/all_gather | solution.py:282
  7.9 59.5 %all-gather.29.cloned.1.call-start = ((), (), s32[]{:S(2)}) async-start(), calls=%async_computation.23 | async-start | bytes 1966080 | tf_op jit(solution)/shard_map/all_gather | solution.py:122
  47.6 41.7 %all-gather.27.cloned.1.call-start = ((), (), s32[]{:S(2)}) async-start(), calls=%async_computation.22 | async-start | bytes 1966080 | tf_op jit(solution)/shard_map/all_gather | solution.py:123
  48.3 62.6 %all-gather.25.cloned.1.call-start = ((), (), s32[]{:S(2)}) async-start(), calls=%async_computation.21 | async-start | bytes 1966080 | tf_op jit(solution)/shard_map/all_gather | solution.py:122
  52.6 79.9 %all-gather.23.cloned.1.call-start = ((), (), s32[]{:S(2)}) async-start(), calls=%async_computation.20 | async-start | bytes 1966080 | tf_op jit(solution)/shard_map/all_gather | solution.py:123
  53.2 103.1 %all-gather.17.cloned.1.call-start = ((), (), s32[]{:S(2)}) async-start(), calls=%async_computation.9 | async-start | bytes 1474560 | tf_op jit(solution)/shard_map/all_gather | solution.py:284
  53.8 136.7 %all-gather.19.cloned.1.call-start = ((), (), s32[]{:S(2)}) async-start(), calls=%async_computation.10 | async-start | bytes 5898240 | tf_op jit(solution)/shard_map/all_gather | solution.py:288
  54.5 174.9 %all-gather.21.cloned.1.call-start = ((), (), s32[]{:S(2)}) async-start(), calls=%async_computation.11 | async-start | bytes 5898240 | tf_op jit(solution)/shard_map/all_gather | solution.py:290
  55.3 284.5 %reduce-scatter.11.cloned.1.call-start = ((), (), s32[]{:S(2)}) async-start(), calls=%async_computation.13 | async-start | bytes 3932160 | tf_op jit(solution)/shard_map/reduce_scatter | solution.py:218
  69.2 92.6 %copy-start.21 = (bf16[1,1024,384]{1,2,0:T(8,128)(2,1)}, bf16[1,1024,384]{1,2,0:T(8,128)(2,1)S(1)}, u32[]{:S(2)}) copy-start(bf16[1,1024,384]{1,2,0:T(8,128)(2,1)S(1)} %copy.85) | copy-start | bytes 2359300
  95.4 63.6 %copy-start.22 = (bf16[1,1024,384]{1,2,0:T(8,128)(2,1)}, bf16[1,1024,384]{1,2,0:T(8,128)(2,1)S(1)}, u32[]{:S(2)}) copy-start(bf16[1,1024,384]{1,2,0:T(8,128)(2,1)S(1)} %copy.88) | copy-start | bytes 2359300
  158.4 90.2 %copy-start.27 = (f32[256,768]{1,0:T(8,128)}, f32[256,768]{1,0:T(8,128)S(1)}, u32[]{:S(2)}) copy-start(f32[256,768]{1,0:T(8,128)S(1)} %get-tuple-element.124) | copy-start | bytes 2359300
  169.3 79.3 %copy-start.11 = (f32[256,768]{1,0:T(8,128)}, f32[256,768]{1,0:T(8,128)S(1)}, u32[]{:S(2)}) copy-start(f32[256,768]{1,0:T(8,128)S(1)} %get-tuple-element.118) | copy-start | bytes 2359300
  169.3 79.3 %copy-start.110 = (f32[256]{0:T(256)}, f32[256]{0:T(256)S(1)}, u32[]{:S(2)}) copy-start(f32[256]{0:T(256)S(1)} %broadcast_multiply_fusion.12) | copy-start | bytes 3076
  169.5 79.0 %copy-start.112 = (f32[256]{0:T(256)}, f32[256]{0:T(256)S(1)}, u32[]{:S(2)}) copy-start(f32[256]{0:T(256)S(1)} %fusion.139) | copy-start | bytes 3076
  169.6 79.0 %copy-start.128 = (f32[256]{0:T(256)}, f32[256]{0:T(256)S(1)}, u32[]{:S(2)}) copy-start(f32[256]{0:T(256)S(1)} %fusion.141) | copy-start | bytes 3076
  169.7 86.7 %copy-start.69 = (f32[6,256]{1,0:T(8,128)}, f32[6,256]{1,0:T(8,128)S(1)}, u32[]{:S(2)}) copy-start(f32[6,256]{1,0:T(8,128)S(1)} %log_add_fusion.3) | copy-start | bytes 18436
  190.4 39.0 %copy-start.18 = (bf16[2,1,256,768]{3,2,1,0:T(8,128)(2,1)S(1)}, bf16[2,1,256,768]{3,2,1,0:T(8,128)(2,1)}, u32[]{:S(2)}) copy-start(bf16[2,1,256,768]{3,2,1,0:T(8,128)(2,1)} %param.29) | copy-start | bytes 2359300
  259.9 81.2 %reduce-scatter.15.cloned.1.call-start = ((), (), s32[]{:S(2)}) async-start(), calls=%async_computation.15 | async-start | bytes 3932160 | tf_op jit(solution)/shard_map/reduce_scatter | solution.py:218
  273.4 104.8 %reduce-scatter.9.cloned.1.call-start = ((), (), s32[]{:S(2)}) async-start(), calls=%async_computation.12 | async-start | bytes 3932160 | tf_op jit(solution)/shard_map/reduce_scatter | solution.py:217
  291.1 127.2 %reduce-scatter.13.cloned.1.call-start = ((), (), s32[]{:S(2)}) async-start(), calls=%async_computation.14 | async-start | bytes 3932160 | tf_op jit(solution)/shard_map/reduce_scatter | solution.py:217
  309.3 137.8 %reduce-scatter.19.cloned.1.call-start = ((), (), s32[]{:S(2)}) async-start(), calls=%async_computation.17 | async-start | bytes 1474560 | tf_op jit(solution)/shard_map/reduce_scatter | solution.py:326
  312.7 184.7 %reduce-scatter.23.cloned.1.call-start = ((), (), s32[]{:S(2)}) async-start(), calls=%async_computation.19 | async-start | bytes 5898240 | tf_op jit(solution)/shard_map/reduce_scatter | solution.py:344
  321.3 226.6 %reduce-scatter.21.cloned.1.call-start = ((), (), s32[]{:S(2)}) async-start(), calls=%async_computation.18 | async-start | bytes 5898240 | tf_op jit(solution)/shard_map/reduce_scatter | solution.py:338
  329.1 261.5 %reduce-scatter.17.cloned.1.call-start = ((), (), s32[]{:S(2)}) async-start(), calls=%async_computation.16 | async-start | bytes 4423680 | tf_op jit(solution)/shard_map/reduce_scatter | solution.py:320
  339.7 107.8 %copy-start.56 = (bf16[6,64,256]{2,1,0:T(8,128)(2,1)}, bf16[6,64,256]{2,1,0:T(8,128)(2,1)S(1)}, u32[]{:S(2)}) copy-start(bf16[6,64,256]{2,1,0:T(8,128)(2,1)S(1)} %fusion.55) | copy-start | bytes 589828
  339.7 79.8 %copy-start.10 = (bf16[2,1,256,768]{3,2,1,0:T(8,128)(2,1)S(1)}, bf16[2,1,256,768]{3,2,1,0:T(8,128)(2,1)}, u32[]{:S(2)}) copy-start(bf16[2,1,256,768]{3,2,1,0:T(8,128)(2,1)} %param.15) | copy-start | bytes 2359300
  339.7 79.8 %copy-start.77 = (f32[768]{0:T(1024)S(1)}, f32[768]{0:T(1024)}, u32[]{:S(2)}) copy-start(f32[768]{0:T(1024)} %copy-done.76) | copy-start | bytes 9220
  339.7 79.8 %copy-start.85 = (f32[768]{0:T(1024)S(1)}, f32[768]{0:T(1024)}, u32[]{:S(2)}) copy-start(f32[768]{0:T(1024)} %copy-done.84) | copy-start | bytes 9220
  339.7 79.8 %copy-start.95 = (f32[256]{0:T(256)S(1)}, f32[256]{0:T(256)}, u32[]{:S(2)}) copy-start(f32[256]{0:T(256)} %copy-done.94) | copy-start | bytes 3076
  339.8 79.8 %copy-start.103 = (f32[256]{0:T(256)S(1)}, f32[256]{0:T(256)}, u32[]{:S(2)}) copy-start(f32[256]{0:T(256)} %copy-done.102) | copy-start | bytes 3076
  479.3 111.3 %copy-start.64 = (bf16[192,768]{1,0:T(8,128)(2,1)S(1)}, bf16[192,768]{1,0:T(8,128)(2,1)}, u32[]{:S(2)}) copy-start(bf16[192,768]{1,0:T(8,128)(2,1)} %reduce-scatter.19.cloned.1.call-done) | copy-start | bytes 884740
  (134 other events, 585.1 us)
Sparse Core Ops, SparseCore 0:
  9.5 33.6 all-gather.14
  47.7 19.6 all-gather.28
  69.6 19.6 all-gather.26
  91.2 19.6 all-gather.24
  112.9 19.6 all-gather.22
  133.9 17.4 all-gather.16
  153.0 37.4 all-gather.18
  192.0 37.4 all-gather.20
  260.0 37.7 reduce-scatter.10
  300.1 37.7 reduce-scatter.14
  340.4 37.7 reduce-scatter.8
  380.6 37.7 reduce-scatter.12
  421.5 25.5 reduce-scatter.18
  449.5 47.9 reduce-scatter.22
  499.9 47.9 reduce-scatter.20
  550.3 40.3 reduce-scatter.16
where the time goes:
time: 893 us; the launch traced here: 887 us
  waiting for transfers between devices  324 us (36%)
  blocking collectives  315 us (35%)
  matrix products  122 us (14%)
  other arithmetic  57.6 us (6%)
  local copies, waits for them, and re-layouts  49.7 us (6%)
  between operations  19.1 us (2%)
    psum x1, blocking collectives, body(): lax.psum((own_ga, own_sa, own_wq, own_bq, own_wo, own_bo, own_gm, own_sm,...  279 us
    reduce_scatter x2, waiting for transfers between devices, layer_pass(): lax.psum_scatter(key_terms, 'shard', scatter_dimension=1, tiled=True)  74.9 us
    reduce_scatter x1, waiting for transfers between devices, body(): lax.psum_scatter(full_wu.astype(jnp.bfloat16), 'shard', scatter_dimension...  50.4 us
    reduce_scatter x1, waiting for transfers between devices, body(): lax.psum_scatter(full_wq.astype(jnp.bfloat16), 'shard', scatter_dimension...  42.8 us
    all_gather x2, waiting for transfers between devices, layer_pass(): lax.all_gather(value_rows, 'shard', axis=1, tiled=True)  37.5 us
    all_gather x1, waiting for transfers between devices, body(): lax.all_gather(weight_down, 'shard', axis=0, tiled=True)  33.4 us
    slice x24, local copies, waits for them, and re-layouts, heads_of(): source[:, :, start_col:start_col + half_columns]  25.6 us
    unnamed x2, blocking collectives  24.7 us
  transfers between devices with their start and end apart: 16, of which 13 were waited for; matrix products, arithmetic and copies ran while one was open for 19% of the time, Pallas kernels for 0%

commit v1 on v0

v1 whole, which is shorter than its diff:
```python
import functools
import math

import jax
import jax.numpy as jnp
from jax import lax
from jax.experimental import pallas as pl
from jax.experimental.pallas import tpu as pltpu
from jax.sharding import PartitionSpec as P

HEADS = 12
DEPTH = 48
PAIR = 128
NN = (((1,), (0,)), ((), ()))
NT = (((1,), (1,)), ((), ()))
TN = (((0,), (0,)), ((), ()))
F32 = jnp.float32
BF16 = jnp.bfloat16


def dot(a, b, dims):
    return lax.dot_general(a, b, dims, preferred_element_type=F32)


def swap_core(x):
    return lax.ppermute(x, "shard", [(s, s ^ 1) for s in range(4)])


def swap_y(x):
    return lax.ppermute(x, "shard", [(s, s ^ 2) for s in range(4)])


def swap_group(x, bit):
    n = lax.axis_size("group")
    return lax.ppermute(x, "group", [(g, g ^ bit) for g in range(n)])


def gather_shard(piece, y, c):
    other = swap_y(piece)
    pair = jnp.where(y == 0, jnp.stack([piece, other]), jnp.stack([other, piece]))
    remote = swap_core(pair)
    first = jnp.where(c == 0, pair, remote)
    second = jnp.where(c == 0, remote, pair)
    return jnp.stack([first, second], axis=1).reshape((4,) + piece.shape)


def pick(x, index, axis):
    return lax.dynamic_index_in_dim(x, index, axis, keepdims=False)


def halves(x, index):
    rows = x.shape[0] // 2
    keep = lax.dynamic_slice_in_dim(x, index * rows, rows, 0)
    send = lax.dynamic_slice_in_dim(x, (1 - index) * rows, rows, 0)
    return keep, send


def reduce_all(full, y, c, group):
    n = lax.axis_size("group")
    full = full.reshape((2, 2) + full.shape[1:])
    held = (pick(full, c, 1).astype(F32) + swap_core(pick(full, 1 - c, 1)).astype(F32)).astype(BF16)
    held = (pick(held, y, 0).astype(F32) + swap_y(pick(held, 1 - y, 0)).astype(F32)).astype(BF16)
    bits = []
    bit = 1
    while bit < n:
        bits.append(bit)
        bit *= 2
    for bit in bits:
        keep, send = halves(held, (group // bit) % 2)
        held = (keep.astype(F32) + swap_group(send, bit).astype(F32)).astype(BF16)
    for bit in reversed(bits):
        other = swap_group(held, bit)
        mine = (group // bit) % 2 == 0
        held = jnp.where(
            mine, jnp.concatenate([held, other], axis=0), jnp.concatenate([other, held], axis=0)
        )
    return held.astype(F32)


def bias_of(qid, kid):
    return jnp.where(kid <= qid, 0.0, -1e30).astype(F32)


def column(row):
    n = row.shape[1]
    return jnp.transpose(jnp.broadcast_to(row, (PAIR, n)))[:, 0:1]


def head_lanes(shape, head):
    lane = lax.broadcasted_iota(jnp.int32, shape, len(shape) - 1)
    return (lane < 64) if head == 0 else (lane >= 64)


def attend_kernel(ids_ref, q_ref, k_ref, kr_ref, v_ref, vr_ref, o_ref, plo_ref, phi_ref, blo, bhi):
    blk = q_ref.shape[0] // 2

    @pl.when(pl.program_id(0) == 0)
    def _():
        own0, own1 = ids_ref[0:1, :], ids_ref[1:2, :]
        rem0, rem1 = ids_ref[2:3, :], ids_ref[3:4, :]
        q0, q1 = column(own0), column(own1)
        blo[...] = jnp.concatenate([bias_of(q0, k) for k in (own0, rem0, rem1)], axis=1)
        bhi[...] = jnp.concatenate([bias_of(q1, k) for k in (own0, rem0, rem1, own1)], axis=1)

    keys = [k_ref[0:blk, :], kr_ref[0:blk, :], kr_ref[blk:, :], k_ref[blk:, :]]
    vals = [v_ref[0:blk, :], vr_ref[0:blk, :], vr_ref[blk:, :], v_ref[blk:, :]]
    for half, (bias, count, p_ref) in enumerate(((blo, 3, plo_ref), (bhi, 4, phi_ref))):
        q = q_ref[half * blk : (half + 1) * blk, :] * BF16(0.125)
        outs = []
        for head in range(2):
            qh = jnp.where(head_lanes(q.shape, head), q, BF16(0))
            s = jnp.concatenate([dot(qh, keys[j], NT) for j in range(count)], axis=1) + bias[...]
            e = jnp.exp(s - jnp.max(s, axis=1, keepdims=True))
            p = (e * (1.0 / jnp.sum(e, axis=1, keepdims=True))).astype(BF16)
            p_ref[head] = p
            acc = None
            for j in range(count):
                t = dot(p[:, j * blk : (j + 1) * blk], vals[j], NN)
                acc = t if acc is None else acc + t
            outs.append(acc)
        o = jnp.where(head_lanes(outs[0].shape, 0), outs[0], outs[1])
        o_ref[half * blk : (half + 1) * blk, :] = o.astype(BF16)


def attend(ids, q, kv, kv_rem):
    rows, feats = q.shape
    blk = rows // 2
    pairs = feats // PAIR
    col = lambda off: pl.BlockSpec((rows, PAIR), lambda i, off=off: (0, i + off))
    return pl.pallas_call(
        attend_kernel,
        grid=(pairs,),
        in_specs=[
            pl.BlockSpec((4, blk), lambda i: (0, 0)),
            col(0),
            col(0),
            col(0),
            col(pairs),
            col(pairs),
        ],
        out_specs=[
            col(0),
            pl.BlockSpec((2, blk, 3 * blk), lambda i: (i, 0, 0)),
            pl.BlockSpec((2, blk, 4 * blk), lambda i: (i, 0, 0)),
        ],
        out_shape=[
            jax.ShapeDtypeStruct((rows, feats), BF16),
            jax.ShapeDtypeStruct((2 * pairs, blk, 3 * blk), BF16),
            jax.ShapeDtypeStruct((2 * pairs, blk, 4 * blk), BF16),
        ],
        scratch_shapes=[pltpu.VMEM((blk, 3 * blk), F32), pltpu.VMEM((blk, 4 * blk), F32)],
        cost_estimate=pl.CostEstimate(
            flops=4 * 7 * blk * blk * feats * 4, transcendentals=7 * blk * blk * 12, bytes_accessed=20 << 20
        ),
        name="attend",
    )(ids, q, kv, kv_rem, kv, kv_rem)


def attend_back_kernel(
    q_ref, k_ref, kr_ref, v_ref, vr_ref, o_ref, g_ref, plo_ref, phi_ref,
    dq_ref, dk_ref, dv_ref, dkr_ref, dvr_ref, acc_k, acc_v,
):
    blk = q_ref.shape[0] // 2
    keys = [k_ref[0:blk, :], kr_ref[0:blk, :], kr_ref[blk:, :], k_ref[blk:, :]]
    vals = [v_ref[0:blk, :], vr_ref[0:blk, :], vr_ref[blk:, :], v_ref[blk:, :]]
    for half, (count, p_ref) in enumerate(((3, plo_ref), (4, phi_ref))):
        span = slice(half * blk, (half + 1) * blk)
        q = q_ref[span, :] * BF16(0.125)
        g = g_ref[span, :]
        og = o_ref[span, :].astype(F32) * g.astype(F32)
        dqs = []
        terms_k = [[] for _ in range(count)]
        terms_v = [[] for _ in range(count)]
        for head in range(2):
            lanes = head_lanes(q.shape, head)
            gh = jnp.where(lanes, g, BF16(0))
            inner = jnp.sum(jnp.where(lanes, og, 0.0), axis=1, keepdims=True)
            acc = None
            for j in range(count):
                p = p_ref[head, :, j * blk : (j + 1) * blk]
                dp = dot(gh, vals[j], NT)
                ds = (p.astype(F32) * (dp - inner)).astype(BF16)
                t = dot(ds, keys[j], NN)
                acc = t if acc is None else acc + t
                terms_k[j].append(dot(ds, q, TN))
                terms_v[j].append(dot(p, g, TN))
            dqs.append(acc)
        lanes = head_lanes(dqs[0].shape, 0)
        dq_ref[span, :] = (jnp.where(lanes, dqs[0], dqs[1]) * 0.125).astype(BF16)
        for j in range(count):
            place = slice(j * blk, (j + 1) * blk)
            tk = jnp.where(lanes, terms_k[j][0], terms_k[j][1])
            tv = jnp.where(lanes, terms_v[j][0], terms_v[j][1])
            if half == 0:
                acc_k[place, :] = tk
                acc_v[place, :] = tv
            elif j == 3:
                dk_ref[blk:, :] = tk.astype(dk_ref.dtype)
                dv_ref[blk:, :] = tv.astype(dv_ref.dtype)
            else:
                tk = acc_k[place, :] + tk
                tv = acc_v[place, :] + tv
                if j == 0:
                    dk_ref[0:blk, :] = tk.astype(dk_ref.dtype)
                    dv_ref[0:blk, :] = tv.astype(dv_ref.dtype)
                else:
                    spot = slice((j - 1) * blk, j * blk)
                    dkr_ref[spot, :] = tk.astype(dkr_ref.dtype)
                    dvr_ref[spot, :] = tv.astype(dvr_ref.dtype)


def attend_back(q, kv, kv_rem, o, g, plo, phi):
    rows, feats = q.shape
    blk = rows // 2
    pairs = feats // PAIR
    col = lambda off: pl.BlockSpec((rows, PAIR), lambda i, off=off: (0, i + off))
    wide = jax.ShapeDtypeStruct((rows, feats), F32)
    low = jax.ShapeDtypeStruct((rows, feats), BF16)
    return pl.pallas_call(
        attend_back_kernel,
        grid=(pairs,),
        in_specs=[
            col(0), col(0), col(0), col(pairs), col(pairs), col(0), col(0),
            pl.BlockSpec((2, blk, 3 * blk), lambda i: (i, 0, 0)),
            pl.BlockSpec((2, blk, 4 * blk), lambda i: (i, 0, 0)),
        ],
        out_specs=[col(0)] * 5,
        out_shape=[low, wide, wide, low, low],
        scratch_shapes=[pltpu.VMEM((3 * blk, PAIR), F32), pltpu.VMEM((3 * blk, PAIR), F32)],
        cost_estimate=pl.CostEstimate(
            flops=8 * 7 * blk * blk * feats * 4, transcendentals=0, bytes_accessed=24 << 20
        ),
        name="attend_back",
    )(q, kv, kv_rem, kv, kv_rem, o, g, plo, phi)


def norm_rows(rows_in, gain_in, shift_in):
    center = jnp.mean(rows_in, axis=-1, keepdims=True)
    deviate = rows_in - center
    spread = jnp.mean(deviate * deviate, axis=-1, keepdims=True)
    return deviate * lax.rsqrt(spread + 1e-05) * gain_in + shift_in


def gelu_tanh(rows_in):
    return (
        0.5
        * rows_in
        * (1.0 + jnp.tanh(0.7978845608028654 * (rows_in + 0.044715 * rows_in * rows_in * rows_in)))
    )


def body(
    inputs, block_ids, attn_gain, attn_shift, weight_qkv, bias_qv, weight_out, bias_out,
    mlp_gain, mlp_shift, weight_up, bias_up, weight_down, bias_down, cotangent,
):
    micro_count, seq_count, blk, feats = inputs.shape
    seq_length = block_ids.shape[2]
    shard = lax.axis_index("shard")
    group = lax.axis_index("group")
    groups = lax.axis_size("group")
    y, c = shard // 2, shard % 2
    ff = 4 * weight_down.shape[0]
    branch = 1.0 / math.sqrt(DEPTH)
    grad_factor = 1.0 / math.sqrt(micro_count * seq_count * seq_length * groups)

    def swap_in(x):
        own = pick(x, y, 0)[0]
        other = swap_y(pick(x, 1 - y, 0)[0])
        return jnp.where(y == 0, jnp.concatenate([own, other]), jnp.concatenate([other, own]))

    def swap_out(rows):
        low, high = rows[:blk], rows[blk:]
        keep = jnp.where(y == 0, low, high)
        other = swap_y(jnp.where(y == 0, high, low))
        return jnp.where(y == 0, jnp.stack([keep, other]), jnp.stack([other, keep]))[:, None]

    vectors = (attn_gain, attn_shift, bias_qv, bias_out, mlp_gain, mlp_shift, bias_up, bias_down)
    sizes = [v.shape[0] for v in vectors]
    width = weight_qkv.shape[1]
    packed = jnp.concatenate(vectors)
    rows_v = -(-packed.shape[0] // width)
    packed = jnp.pad(packed, (0, rows_v * width - packed.shape[0])).reshape(rows_v, width)
    first_pack = jnp.concatenate([weight_qkv, jnp.pad(packed, ((0, 8 - rows_v), (0, 0)))], axis=0)
    x = swap_in(inputs)
    pack_a = gather_shard(first_pack, y, c)
    slice_rows = weight_qkv.shape[0]
    w_qkv = pack_a[:, :slice_rows].reshape(feats, width)
    vec_rows = pack_a[:, slice_rows : slice_rows + rows_v].reshape(4, rows_v * width).astype(F32)
    full_vectors = []
    at = 0
    for size in sizes:
        full_vectors.append(vec_rows[:, at : at + size].reshape(4 * size))
        at += size
    ga, sa, bqv, bo, gm, sm, bu, bd = full_vectors
    pack_b = gather_shard(jnp.concatenate([weight_out, weight_up], axis=1), y, c)
    w_out = pack_b[:, :, :feats].reshape(feats, feats)
    w_up = pack_b[:, :, feats:].reshape(feats, ff)
    w_down = gather_shard(weight_down, y, c).reshape(ff, feats)
    cot = swap_in(cotangent)

    ids_seq = pick(block_ids, y, 0)[0].astype(F32).reshape(4, blk)
    order = jnp.where(c == 0, jnp.array([0, 2, 1, 3]), jnp.array([1, 3, 0, 2]))
    ids = jnp.concatenate([pick(ids_seq, order[i], 0)[None] for i in range(4)], axis=0)

    tokens = x.astype(F32)
    first = norm_rows(tokens, ga, sa).astype(BF16)
    full_bias = jnp.concatenate([bqv[:feats], jnp.zeros((feats,), F32), bqv[feats:]])
    mixed = (jnp.dot(first, w_qkv, preferred_element_type=F32) + full_bias).astype(BF16)
    q, kv = mixed[:, :feats], mixed[:, feats:]
    kv_rem = swap_core(kv)
    attended, plo, phi = attend(ids, q, kv, kv_rem)
    residual = tokens + branch * (jnp.dot(attended, w_out, preferred_element_type=F32) + bo)
    second = norm_rows(residual, gm, sm).astype(BF16)
    pre = jnp.dot(second, w_up, preferred_element_type=F32) + bu
    hidden = gelu_tanh(pre).astype(BF16)
    closing = jnp.dot(hidden, w_down, preferred_element_type=F32) + bd
    out_rows = (residual + branch * closing).astype(BF16)
    outputs = swap_out(out_rows)

    gout = cot.astype(F32)
    g_final = (branch * gout).astype(BF16)
    gw_down = dot(hidden, g_final, TN).astype(BF16)
    own_down = reduce_all(gw_down.reshape(4, ff // 4, feats), y, c, group)
    _, gelu_pull = jax.vjp(gelu_tanh, pre)
    g_pre = gelu_pull(dot(g_final, w_down, NT))[0].astype(BF16)
    gw_up = dot(second, g_pre, TN).astype(BF16)
    g_second = dot(g_pre, w_up, NT)
    _, norm_pull = jax.vjp(norm_rows, residual, gm, sm)
    g_res_part, g_gm, g_sm = norm_pull(g_second)
    g_res = gout + g_res_part
    g_attn = (branch * g_res).astype(BF16)
    gw_out = dot(attended, g_attn, TN).astype(BF16)
    own_mid = reduce_all(
        jnp.concatenate(
            [gw_out.reshape(4, slice_rows, feats), gw_up.reshape(4, slice_rows, ff)], axis=2
        ),
        y, c, group,
    )
    g_att = dot(g_attn, w_out, NT).astype(BF16)
    dq, dk, dv, dkr, dvr = attend_back(q, kv, kv_rem, attended, g_att, plo, phi)
    far = swap_core(jnp.concatenate([dkr, dvr], axis=1)).astype(F32)
    g_mixed = jnp.concatenate(
        [dq, (dk + far[:, :feats]).astype(BF16), (dv + far[:, feats:]).astype(BF16)], axis=1
    )
    g_first = dot(g_mixed, w_qkv, NT)
    _, first_pull = jax.vjp(norm_rows, tokens, ga, sa)
    g_tok, g_ga, g_sa = first_pull(g_first)
    g_inputs = swap_out((g_res + g_tok).astype(BF16)).astype(F32)
    gw_qkv = dot(first, g_mixed, TN).astype(BF16)
    mixed_sums = jnp.sum(g_mixed.astype(F32), axis=0)
    vec_grads = (
        g_ga, g_sa, jnp.concatenate([mixed_sums[:feats], mixed_sums[2 * feats :]]),
        jnp.sum(g_attn.astype(F32), axis=0), g_gm, g_sm,
        jnp.sum(g_pre.astype(F32), axis=0), jnp.sum(g_final.astype(F32), axis=0),
    )
    vec_pack = jnp.concatenate([v.reshape(4, -1) for v in vec_grads], axis=1)
    vec_pack = jnp.pad(vec_pack, ((0, 0), (0, rows_v * width - vec_pack.shape[1])))
    vec_pack = vec_pack.reshape(4, rows_v, width).astype(BF16)
    step = 2 * groups
    pad = -(slice_rows + rows_v) % step
    vec_pack = jnp.pad(vec_pack, ((0, 0), (0, pad), (0, 0)))
    own_last = reduce_all(
        jnp.concatenate([gw_qkv.reshape(4, slice_rows, width), vec_pack], axis=1), y, c, group
    )
    own_qkv = own_last[:slice_rows]
    own_vec = own_last[slice_rows : slice_rows + rows_v].reshape(-1) * grad_factor
    vecs = []
    at = 0
    for size in sizes:
        vecs.append(own_vec[at : at + size])
        at += size
    own_mid = own_mid * grad_factor
    return (
        outputs, g_inputs, vecs[0], vecs[1], own_qkv * grad_factor, vecs[2],
        own_mid[:, :feats], vecs[3], vecs[4], vecs[5], own_mid[:, feats:], vecs[6],
        own_down * grad_factor, vecs[7],
    )


def solution(mesh):
    row = P("shard", None)
    vec = P("shard")
    big = P(None, "group", "shard", None)
    in_specs = (
        big, P(None, "group", None), vec, vec, row, vec, row, vec, vec, vec, row, vec, row, vec, big,
    )
    out_specs = (big, big, vec, vec, row, vec, row, vec, vec, vec, row, vec, row, vec)
    return jax.shard_map(body, mesh=mesh, in_specs=in_specs, out_specs=out_specs, check_vma=False)
```

time: 893 us -> 446 us (0.50)
  blocking collectives: 315 us -> 0 us
  waiting for transfers between devices: 324 us -> 193 us
  matrix products: 122 us -> 46.9 us
  starting transfers between devices: 0.64 us -> 49.9 us
  Pallas kernels: 0 us -> 46.4 us
  local copies, waits for them, and re-layouts: 49.7 us -> 35.5 us
  between operations: 19.1 us -> 10.1 us
    psum x1 -> x0, blocking collectives: 279 us -> none  [body(): lax.psum((own_ga, own_sa, own_wq, own_bq, own_wo, own_bo, own_gm, own_sm,...]
    reduce_scatter x8 -> x0, waiting for transfers between devices: 205 us -> none  [the longest x2 74.9 us: layer_pass(): lax.psum_scatter(key_terms, 'shard', scatter_dimension=1, tiled=True)]
    ppermute x0 -> x36, waiting for transfers between devices: none -> 193 us  [the longest x10 129 us: swap_y(): return lax.ppermute(x, 'shard', [(s, s ^ 2) for s in range(4)])]
    all_gather x8 -> x0, waiting for transfers between devices: 115 us -> none  [the longest x2 37.5 us: layer_pass(): lax.all_gather(value_rows, 'shard', axis=1, tiled=True)]
    dot_general x48 -> x12, matrix products: 122 us -> 46.9 us  [the longest x8 34.9 us: dot(): return lax.dot_general(a, b, dims, preferred_element_type=F32)]
    ppermute x0 -> x36, starting transfers between devices: none -> 49.9 us  [the longest x18 36 us: swap_group(): return lax.ppermute(x, 'group', [(g, g ^ bit) for g in range(n)])]
    pallas_call x0 -> x2, Pallas kernels: none -> 46.4 us  [the longest x1 28.9 us: attend_back(): pl.pallas_call(attend_back_kernel, grid=(pairs,), in_specs=[col(0), col(0...]
    unnamed x2 -> x0, blocking collectives: 24.7 us -> none
  transfers between devices with their start and end apart: 16 -> 36, of which waited for: 13 -> 21; matrix products, arithmetic and copies ran while one was open for 19% -> 22% of each run, Pallas kernels for 0% -> 10%
where the time goes in v1:
time: 446 us; the launch traced here: 443 us
  waiting for transfers between devices  193 us (43%)
  other arithmetic  61.7 us (14%)
  starting transfers between devices  49.9 us (11%)
  matrix products  46.9 us (11%)
  Pallas kernels  46.4 us (10%)
  local copies, waits for them, and re-layouts  35.5 us (8%)
  between operations  10.1 us (2%)
    ppermute x10, waiting for transfers between devices, swap_y(): return lax.ppermute(x, 'shard', [(s, s ^ 2) for s in range(4)])  129 us
    ppermute x18, waiting for transfers between devices, swap_group(): return lax.ppermute(x, 'group', [(g, g ^ bit) for g in range(n)])  63.9 us
    ppermute x18, starting transfers between devices, swap_group(): return lax.ppermute(x, 'group', [(g, g ^ bit) for g in range(n)])  36 us
    dot_general x8, matrix products, dot(): return lax.dot_general(a, b, dims, preferred_element_type=F32)  34.9 us
    pallas_call x1, Pallas kernels, attend_back(): pl.pallas_call(attend_back_kernel, grid=(pairs,), in_specs=[col(0), col(0...  28.9 us
    pallas_call x1, Pallas kernels, attend(): pl.pallas_call(attend_kernel, grid=(pairs,), in_specs=[pl.BlockSpec((4, b...  17.5 us
    ppermute x10, starting transfers between devices, swap_y(): return lax.ppermute(x, 'shard', [(s, s ^ 2) for s in range(4)])  12.7 us
    another operation x6, other arithmetic, gather_shard(): return jnp.stack([first, second], axis=1).reshape((4,) + piece.shape)  12.5 us
  transfers between devices with their start and end apart: 36, of which 21 were waited for; matrix products, arithmetic and copies ran while one was open for 22% of the time, Pallas kernels for 10%

profile of v1, /device:TPU:0, one launch (start us, length us, event | category | flops | bytes accessed | tf_op | source)
XLA Modules:
  0.0 443.2 jit_solution(9561059591900465793)
XLA Ops:
  0.7 5.5 %concatenate.166 = bf16[2304]{0:T(1024)(128)(2,1)S(1)} concatenate(bf16[192]{0:T(256)(128)(2,1)} %param.19, bf16[192]{0:T(256)(128)(2,1)} %param.20, bf16[384]{0:T(512)(128)(2,1)} %param.22, bf16[192]{0:T(256)(128)(2,1)} %param.24, bf16[192]{0:T(256)(128)(2,1)} %param.25, bf16[192]{0:T(256)(128)(2,1)} %param.26, bf16[768]{0:T(1024)(128)(2,1)} %param.28, bf16[192]{0:T(256)(128)(2,1)} %param.30), dimensions={0} | concatenate | bytes 9216 | tf_op jit(solution)/shard_map/concatenate | solution.py:280
  16.7 16.3 %collective-permute-done.1 = bf16[200,2304]{1,0:T(8,128)(2,1)} collective-permute-done((bf16[200,2304]{1,0:T(8,128)(2,1)}, bf16[200,2304]{1,0:T(8,128)(2,1)}, u32[]{:S(2)}, u32[]{:S(2)}) %collective-permute-start.1) | collective-permute-done | bytes 921632 | tf_op jit(solution)/shard_map/ppermute | solution.py:30
  36.0 5.3 %collective-permute-done = bf16[256,768]{1,0:T(8,128)(2,1)S(1)} collective-permute-done((bf16[256,768]{1,0:T(8,128)(2,1)}, bf16[256,768]{1,0:T(8,128)(2,1)S(1)}, u32[]{:S(2)}, u32[]{:S(2)}) %collective-permute-start) | collective-permute-done | bytes 393248 | tf_op jit(solution)/shard_map/ppermute | solution.py:30
  42.1 55.4 %collective-permute-done.6 = bf16[768,768]{1,0:T(8,128)(2,1)} collective-permute-done((bf16[768,768]{1,0:T(8,128)(2,1)}, bf16[768,768]{1,0:T(8,128)(2,1)}, u32[]{:S(2)}, u32[]{:S(2)}) %collective-permute-start.6) | collective-permute-done | bytes 1179680 | tf_op jit(solution)/shard_map/ppermute | solution.py:30
  97.5 4.3 maximum_select_fusion.1
  101.8 4.0 maximum_select_fusion
  111.4 4.3 fusion.8
  132.0 3.6 select_bitcast_fusion.3
  138.1 17.5 %attend.1 = (bf16[512,768]{1,0:T(8,128)(2,1)}, bf16[12,256,768]{2,1,0:T(8,128)(2,1)}, bf16[12,256,1024]{2,1,0:T(8,128)(2,1)}) custom-call(f32[4,256]{1,0:T(4,128)} %pad_maximum_fusion.6.ids_ref, bf16[512,768]{1,0:T(8,128)(2,1)} %slice.229.q_ref, bf16[512,1536]{1,0:T(8,128)(2,1)} %slice.230.k_ref.v_ref, ...), custom_call_target="tpu_custom_call" | custom-call | flops 5637144576 | bytes 20971520 | tf_op jit(solution)/shard_map/attend/pallas_call | solution.py:130
  155.7 3.1 select_bitcast_fusion.1
  164.7 10.6 %fusion.67 = (bf16[3072]{0:T(1024)(128)(2,1)}, bf16[512,3072]{1,0:T(8,128)(2,1)S(1)}) fusion(bf16[3072,768]{1,0:T(8,128)(2,1)S(1)} %bitcast.143, bf16[256,768]{1,0:T(8,128)(2,1)S(1)} %get-tuple-element.54, bf16[256,768]{1,0:T(8,128)(2,1)S(1)} %collective-permute-done.9, pred[]{:T(512)S(6)} %eq.57, f32[512,3072]{1,0:T(8,128)S(1)} %fusion.57, f32[3072]{0:T(1024)S(1)} %add.311), kind=kOutput, calls=%fused_computation.187 | convolution fusion | flops 2461529088 | bytes 14960641 | tf_op jit(solution)/shard_map/dot_general | solution.py:22
  175.3 3.5 multiply_reduce_fusion
  178.8 4.8 %convolution_convert_fusion.1 = bf16[768,3072]{1,0:T(8,128)(2,1)} fusion(bf16[512,3072]{1,0:T(8,128)(2,1)S(1)} %get-tuple-element.89, f32[512,768]{1,0:T(8,128)S(1)} %get-tuple-element.85, f32[768]{0:T(1024)S(1)} %add.308, f32[768]{0:T(1024)S(1)} %mul.277, f32[512]{0:T(512)S(1)} %fusion.48, f32[512]{0:T(512)S(1)} %broadcast_multiply_fusion), kind=kOutput, calls=%fused_computation.21 | convolution fusion | flops 2420244480 | bytes 9447424 | tf_op jit(solution)/shard_map/dot_general | solution.py:22
  188.3 4.0 add_convert_fusion.1
  193.5 28.9 %attend_back.1 = (bf16[512,768]{1,0:T(8,128)(2,1)}, f32[512,768]{1,0:T(8,128)}, f32[512,768]{1,0:T(8,128)}, bf16[512,768]{1,0:T(8,128)(2,1)}, bf16[512,768]{1,0:T(8,128)(2,1)}) custom-call(bf16[512,768]{1,0:T(8,128)(2,1)} %slice.229.q_ref, bf16[512,1536]{1,0:T(8,128)(2,1)} %slice.230.k_ref.v_ref, bf16[512,1536]{1,0:T(8,128)(2,1)} %collective-permute-done.3.kr_ref.vr_ref, ...), custom_call_target="tpu_custom_call" | custom-call | flops 11274289152 | bytes 25165824 | tf_op jit(solution)/shard_map/attend_back/pallas_call | solution.py:219
  229.6 3.6 fusion.11
  233.7 7.0 %convolution_convert_fusion = bf16[3072,768]{1,0:T(8,128)(2,1)S(1)} fusion(bf16[256,768]{1,0:T(8,128)(2,1)S(1)} %copy-done.13, bf16[256,768]{1,0:T(8,128)(2,1)S(1)} %copy-done.5, pred[]{:T(512)S(6)} %eq.57, f32[512,3072]{1,0:T(8,128)} %copy-done.41, f32[3072]{0:T(1024)S(1)} %copy-done.30), kind=kOutput, calls=%fused_computation.20 | convolution fusion | flops 2438725632 | bytes 11808769 | tf_op jit(solution)/shard_map/dot_general | solution.py:22
  263.9 3.8 convolution_convert_fusion.2
  280.2 24.0 %collective-permute-done.29 = bf16[768,768]{1,0:T(8,128)(2,1)S(1)} collective-permute-done((bf16[768,768]{1,0:T(8,128)(2,1)S(1)}, bf16[768,768]{1,0:T(8,128)(2,1)S(1)}, u32[]{:S(2)}, u32[]{:S(2)}) %collective-permute-start.29) | collective-permute-done | bytes 1179680 | tf_op jit(solution)/shard_map/ppermute | solution.py:30
  306.8 10.5 %collective-permute-done.30 = bf16[384,768]{1,0:T(8,128)(2,1)S(1)} collective-permute-done((bf16[384,768]{1,0:T(8,128)(2,1)S(1)}, bf16[384,768]{1,0:T(8,128)(2,1)S(1)}, u32[]{:S(2)}, u32[]{:S(2)}) %collective-permute-start.30) | collective-permute-done | bytes 589856 | tf_op jit(solution)/shard_map/ppermute | solution.py:35
  321.1 4.6 %collective-permute-done.31 = bf16[192,768]{1,0:T(8,128)(2,1)S(1)} collective-permute-done((bf16[192,768]{1,0:T(8,128)(2,1)S(1)}, bf16[192,768]{1,0:T(8,128)(2,1)S(1)}, u32[]{:S(2)}, u32[]{:S(2)}) %collective-permute-start.31) | collective-permute-done | bytes 294944 | tf_op jit(solution)/shard_map/ppermute | solution.py:35
  325.8 3.1 collective-permute-start.32
  328.9 6.9 %collective-permute-done.21 = bf16[192,3840]{1,0:T(8,128)(2,1)S(1)} collective-permute-done((bf16[192,3840]{1,0:T(8,128)(2,1)S(1)}, bf16[192,3840]{1,0:T(8,128)(2,1)S(1)}, u32[]{:S(2)}, u32[]{:S(2)}) %collective-permute-start.21) | collective-permute-done | bytes 1474592 | tf_op jit(solution)/shard_map/ppermute | solution.py:30
  336.2 18.8 %collective-permute-done.13 = bf16[208,2304]{1,0:T(8,128)(2,1)S(1)} collective-permute-done((bf16[208,2304]{1,0:T(8,128)(2,1)S(1)}, bf16[208,2304]{1,0:T(8,128)(2,1)S(1)}, u32[]{:S(2)}, u32[]{:S(2)}) %collective-permute-start.13) | collective-permute-done | bytes 958496 | tf_op jit(solution)/shard_map/ppermute | solution.py:30
  360.5 5.1 %collective-permute-done.33 = bf16[96,768]{1,0:T(8,128)(2,1)S(1)} collective-permute-done((bf16[96,768]{1,0:T(8,128)(2,1)S(1)}, bf16[96,768]{1,0:T(8,128)(2,1)S(1)}, u32[]{:S(2)}, u32[]{:S(2)}) %collective-permute-start.33) | collective-permute-done | bytes 147488 | tf_op jit(solution)/shard_map/ppermute | solution.py:35
  371.3 4.2 collective-permute-done.34
  376.2 8.8 %collective-permute-done.22 = bf16[96,3840]{1,0:T(8,128)(2,1)S(1)} collective-permute-done((bf16[96,3840]{1,0:T(8,128)(2,1)S(1)}, bf16[96,3840]{1,0:T(8,128)(2,1)S(1)}, u32[]{:S(2)}, u32[]{:S(2)}) %collective-permute-start.22) | collective-permute-done | bytes 737312 | tf_op jit(solution)/shard_map/ppermute | solution.py:35
  389.9 4.1 collective-permute-done.16
  401.9 4.9 %collective-permute-start.18 = (bf16[52,2304]{1,0:T(8,128)(2,1)S(1)}, bf16[52,2304]{1,0:T(8,128)(2,1)S(1)}, u32[]{:S(2)}, u32[]{:S(2)}) collective-permute-start(bf16[52,2304]{1,0:T(8,128)(2,1)S(1)} %maximum_select_fusion.15), channel_id=1, source_target_pairs={{0,8},{4,12},{8,0},{12,4},{16,24},{20,28},{24,16},{28,20},{1,9},{5... | collective-permute-start | bytes 718856 | tf_op jit(solution)/shard_map/ppermute | solution.py:35
  406.8 5.2 %collective-permute-done.24 = bf16[24,3840]{1,0:T(8,128)(2,1)S(1)} collective-permute-done((bf16[24,3840]{1,0:T(8,128)(2,1)S(1)}, bf16[24,3840]{1,0:T(8,128)(2,1)S(1)}, u32[]{:S(2)}, u32[]{:S(2)}) %collective-permute-start.24) | collective-permute-done | bytes 184352 | tf_op jit(solution)/shard_map/ppermute | solution.py:35
  412.4 4.5 %collective-permute-start.19 = (bf16[104,2304]{1,0:T(8,128)(2,1)S(1)}, bf16[104,2304]{1,0:T(8,128)(2,1)S(1)}, u32[]{:S(2)}, u32[]{:S(2)}) collective-permute-start(bf16[104,2304]{1,0:T(8,128)(2,1)S(1)} %maximum_select_fusion.12), channel_id=1, source_target_pairs={{0,4},{4,0},{8,12},{12,8},{16,20},{20,16},{24,28},{28,24},{1,5},{5... | collective-permute-start | bytes 1437704 | tf_op jit(solution)/shard_map/ppermute | solution.py:35
  430.7 9.3 %collective-permute-done.27 = bf16[96,3840]{1,0:T(8,128)(2,1)S(1)} collective-permute-done((bf16[96,3840]{1,0:T(8,128)(2,1)S(1)}, bf16[96,3840]{1,0:T(8,128)(2,1)S(1)}, u32[]{:S(2)}, u32[]{:S(2)}) %collective-permute-start.27) | collective-permute-done | bytes 737312 | tf_op jit(solution)/shard_map/ppermute | solution.py:35
  (281 shorter events, 133.6 us)
Async XLA Ops:
  8.4 24.6 %collective-permute-start.1 = (bf16[200,2304]{1,0:T(8,128)(2,1)}, bf16[200,2304]{1,0:T(8,128)(2,1)}, u32[]{:S(2)}, u32[]{:S(2)}) collective-permute-start(bf16[200,2304]{1,0:T(8,128)(2,1)} %get-tuple-element.50), channel_id=1, source_target_pairs={{0,2},{1,3},{2,0},{3,1},{4,6},{5,7},{6,4},{7,5},{8,10},{9,11},{10,... | collective-permute-start | bytes 2764808 | tf_op jit(solution)/shard_map/ppermute | solution.py:30
  12.2 29.1 %collective-permute-start = (bf16[256,768]{1,0:T(8,128)(2,1)}, bf16[256,768]{1,0:T(8,128)(2,1)S(1)}, u32[]{:S(2)}, u32[]{:S(2)}) collective-permute-start(bf16[256,768]{1,0:T(8,128)(2,1)} %get-tuple-element.58), channel_id=1, source_target_pairs={{0,2},{1,3},{2,0},{3,1},{4,6},{5,7},{6,4},{7,5},{8,10},{9,11},{10,... | collective-permute-start | bytes 1179656 | tf_op jit(solution)/shard_map/ppermute | solution.py:30
  14.5 87.2 %collective-permute-start.4 = (bf16[192,3840]{1,0:T(8,128)(2,1)S(1)}, bf16[192,3840]{1,0:T(8,128)(2,1)}, u32[]{:S(2)}, u32[]{:S(2)}) collective-permute-start(bf16[192,3840]{1,0:T(8,128)(2,1)S(1)} %constant_dynamic-update-slice_fusion), channel_id=1, source_target_pairs={{0,2},{1,3},{2,0},{3,1},{4,6},{5,7},{6,4},{7,5},{8,10},{9,11},{10,... | collective-permute-start | bytes 4423688 | tf_op jit(solution)/shard_map/ppermute | solution.py:30
  16.6 80.8 %collective-permute-start.6 = (bf16[768,768]{1,0:T(8,128)(2,1)}, bf16[768,768]{1,0:T(8,128)(2,1)}, u32[]{:S(2)}, u32[]{:S(2)}) collective-permute-start(bf16[768,768]{1,0:T(8,128)(2,1)} %param.29), channel_id=1, source_target_pairs={{0,2},{1,3},{2,0},{3,1},{4,6},{5,7},{6,4},{7,5},{8,10},{9,11},{10,... | collective-permute-start | bytes 3538952 | tf_op jit(solution)/shard_map/ppermute | solution.py:30
  36.0 70.2 %collective-permute-start.2 = (bf16[2,200,2304]{2,1,0:T(8,128)(2,1)}, bf16[2,200,2304]{2,1,0:T(8,128)(2,1)}, u32[]{:S(2)}, u32[]{:S(2)}) collective-permute-start(bf16[2,200,2304]{2,1,0:T(8,128)(2,1)} %maximum_select_fusion.2), channel_id=1, source_target_pairs={{0,1},{1,0},{2,3},{3,2},{4,5},{5,4},{6,7},{7,6},{8,9},{9,8},{10,11... | collective-permute-start | bytes 5529608 | tf_op jit(solution)/shard_map/ppermute | solution.py:26
  101.8 30.2 %collective-permute-start.7 = (bf16[2,768,768]{2,1,0:T(8,128)(2,1)}, bf16[2,768,768]{2,1,0:T(8,128)(2,1)}, u32[]{:S(2)}, u32[]{:S(2)}) collective-permute-start(bf16[2,768,768]{2,1,0:T(8,128)(2,1)} %maximum_select_fusion.1), channel_id=1, source_target_pairs={{0,1},{1,0},{2,3},{3,2},{4,5},{5,4},{6,7},{7,6},{8,9},{9,8},{10,11... | collective-permute-start | bytes 7077896 | tf_op jit(solution)/shard_map/ppermute | solution.py:26
  105.8 49.9 %collective-permute-start.5 = (bf16[2,192,3840]{2,1,0:T(8,128)(2,1)}, bf16[2,192,3840]{2,1,0:T(8,128)(2,1)}, u32[]{:S(2)}, u32[]{:S(2)}) collective-permute-start(bf16[2,192,3840]{2,1,0:T(8,128)(2,1)} %maximum_select_fusion), channel_id=1, source_target_pairs={{0,1},{1,0},{2,3},{3,2},{4,5},{5,4},{6,7},{7,6},{8,9},{9,8},{10,11... | collective-permute-start | bytes 8847368 | tf_op jit(solution)/shard_map/ppermute | solution.py:26
  117.6 20.5 %collective-permute-start.3 = (bf16[512,1536]{1,0:T(8,128)(2,1)}, bf16[512,1536]{1,0:T(8,128)(2,1)}, u32[]{:S(2)}, u32[]{:S(2)}) collective-permute-start(bf16[512,1536]{1,0:T(8,128)(2,1)} %slice.230.k_ref.v_ref), channel_id=1, source_target_pairs={{0,1},{1,0},{2,3},{3,2},{4,5},{5,4},{6,7},{7,6},{8,9},{9,8},{10,11... | collective-permute-start | bytes 4718600 | tf_op jit(solution)/shard_map/ppermute | solution.py:26
  118.4 46.2 %collective-permute-start.9 = (bf16[256,768]{1,0:T(8,128)(2,1)}, bf16[256,768]{1,0:T(8,128)(2,1)S(1)}, u32[]{:S(2)}, u32[]{:S(2)}) collective-permute-start(bf16[256,768]{1,0:T(8,128)(2,1)} %get-tuple-element.55), channel_id=1, source_target_pairs={{0,2},{1,3},{2,0},{3,1},{4,6},{5,7},{6,4},{7,5},{8,10},{9,11},{10,... | collective-permute-start | bytes 1179656 | tf_op jit(solution)/shard_map/ppermute | solution.py:30
  193.2 50.4 %collective-permute-start.8 = (bf16[256,768]{1,0:T(8,128)(2,1)}, bf16[256,768]{1,0:T(8,128)(2,1)}, u32[]{:S(2)}, u32[]{:S(2)}) collective-permute-start(bf16[256,768]{1,0:T(8,128)(2,1)} %get-tuple-element.57), channel_id=1, source_target_pairs={{0,2},{1,3},{2,0},{3,1},{4,6},{5,7},{6,4},{7,5},{8,10},{9,11},{10,... | collective-permute-start | bytes 1179656 | tf_op jit(solution)/shard_map/ppermute | solution.py:30
  225.0 20.7 %collective-permute-start.10 = (bf16[512,1536]{1,0:T(8,128)(2,1)}, bf16[512,1536]{1,0:T(8,128)(2,1)}, u32[]{:S(2)}, u32[]{:S(2)}) collective-permute-start(bf16[512,1536]{1,0:T(8,128)(2,1)} %pad_maximum_fusion.4), channel_id=1, source_target_pairs={{0,1},{1,0},{2,3},{3,2},{4,5},{5,4},{6,7},{7,6},{8,9},{9,8},{10,11... | collective-permute-start | bytes 4718600 | tf_op jit(solution)/shard_map/ppermute | solution.py:26
  233.2 43.9 %collective-permute-start.20 = (bf16[2,192,3840]{2,1,0:T(8,128)(2,1)}, bf16[2,192,3840]{2,1,0:T(8,128)(2,1)}, u32[]{:S(2)}, u32[]{:S(2)}) collective-permute-start(bf16[2,192,3840]{2,1,0:T(8,128)(2,1)} %fusion.11), channel_id=1, source_target_pairs={{0,1},{1,0},{2,3},{3,2},{4,5},{5,4},{6,7},{7,6},{8,9},{9,8},{10,11... | collective-permute-start | bytes 8847368 | tf_op jit(solution)/shard_map/ppermute | solution.py:26
  243.6 29.3 %collective-permute-start.28 = (bf16[2,768,768]{2,1,0:T(8,128)(2,1)}, bf16[2,768,768]{2,1,0:T(8,128)(2,1)}, u32[]{:S(2)}, u32[]{:S(2)}) collective-permute-start(bf16[2,768,768]{2,1,0:T(8,128)(2,1)} %dynamic-slice_bitcast_fusion), channel_id=1, source_target_pairs={{0,1},{1,0},{2,3},{3,2},{4,5},{5,4},{6,7},{7,6},{8,9},{9,8},{10,11... | collective-permute-start | bytes 7077896 | tf_op jit(solution)/shard_map/ppermute | solution.py:26
  258.5 11.8 %collective-permute-start.11 = (bf16[256,768]{1,0:T(8,128)(2,1)}, bf16[256,768]{1,0:T(8,128)(2,1)}, u32[]{:S(2)}, u32[]{:S(2)}) collective-permute-start(bf16[256,768]{1,0:T(8,128)(2,1)} %get-tuple-element.53), channel_id=1, source_target_pairs={{0,2},{1,3},{2,0},{3,1},{4,6},{5,7},{6,4},{7,5},{8,10},{9,11},{10,... | collective-permute-start | bytes 1179656 | tf_op jit(solution)/shard_map/ppermute | solution.py:30
  267.9 38.5 %collective-permute-start.12 = (bf16[2,208,2304]{2,1,0:T(8,128)(2,1)S(1)}, bf16[2,208,2304]{2,1,0:T(8,128)(2,1)S(1)}, u32[]{:S(2)}, u32[]{:S(2)}) collective-permute-start(bf16[2,208,2304]{2,1,0:T(8,128)(2,1)S(1)} %fusion.21), channel_id=1, source_target_pairs={{0,1},{1,0},{2,3},{3,2},{4,5},{5,4},{6,7},{7,6},{8,9},{9,8},{10,11... | collective-permute-start | bytes 5750792 | tf_op jit(solution)/shard_map/ppermute | solution.py:26
  275.3 28.9 %collective-permute-start.29 = (bf16[768,768]{1,0:T(8,128)(2,1)S(1)}, bf16[768,768]{1,0:T(8,128)(2,1)S(1)}, u32[]{:S(2)}, u32[]{:S(2)}) collective-permute-start(bf16[768,768]{1,0:T(8,128)(2,1)S(1)} %dynamic-slice_bitcast_fusion.2), channel_id=1, source_target_pairs={{0,2},{1,3},{2,0},{3,1},{4,6},{5,7},{6,4},{7,5},{8,10},{9,11},{10,... | collective-permute-start | bytes 3538952 | tf_op jit(solution)/shard_map/ppermute | solution.py:30
  279.8 56.0 %collective-permute-start.21 = (bf16[192,3840]{1,0:T(8,128)(2,1)S(1)}, bf16[192,3840]{1,0:T(8,128)(2,1)S(1)}, u32[]{:S(2)}, u32[]{:S(2)}) collective-permute-start(bf16[192,3840]{1,0:T(8,128)(2,1)S(1)} %dynamic-slice_bitcast_fusion.1), channel_id=1, source_target_pairs={{0,2},{1,3},{2,0},{3,1},{4,6},{5,7},{6,4},{7,5},{8,10},{9,11},{10,... | collective-permute-start | bytes 4423688 | tf_op jit(solution)/shard_map/ppermute | solution.py:30
  304.6 12.8 %collective-permute-start.30 = (bf16[384,768]{1,0:T(8,128)(2,1)S(1)}, bf16[384,768]{1,0:T(8,128)(2,1)S(1)}, u32[]{:S(2)}, u32[]{:S(2)}) collective-permute-start(bf16[384,768]{1,0:T(8,128)(2,1)S(1)} %constant_dynamic-slice_fusion.2), channel_id=1, source_target_pairs={{0,4},{4,0},{8,12},{12,8},{16,20},{20,16},{24,28},{28,24},{1,5},{5... | collective-permute-start | bytes 1769480 | tf_op jit(solution)/shard_map/ppermute | solution.py:35
  319.5 35.5 %collective-permute-start.13 = (bf16[208,2304]{1,0:T(8,128)(2,1)S(1)}, bf16[208,2304]{1,0:T(8,128)(2,1)S(1)}, u32[]{:S(2)}, u32[]{:S(2)}) collective-permute-start(bf16[208,2304]{1,0:T(8,128)(2,1)S(1)} %dynamic-slice_bitcast_fusion.3), channel_id=1, source_target_pairs={{0,2},{1,3},{2,0},{3,1},{4,6},{5,7},{6,4},{7,5},{8,10},{9,11},{10,... | collective-permute-start | bytes 2875400 | tf_op jit(solution)/shard_map/ppermute | solution.py:30
  325.8 31.3 %collective-permute-start.32 = (bf16[96,768]{1,0:T(8,128)(2,1)S(1)}, bf16[96,768]{1,0:T(8,128)(2,1)S(1)}, u32[]{:S(2)}, u32[]{:S(2)}) collective-permute-start(bf16[96,768]{1,0:T(8,128)(2,1)S(1)} %constant_dynamic-slice_fusion), channel_id=1, source_target_pairs={{0,16},{4,20},{8,24},{12,28},{16,0},{20,4},{24,8},{28,12},{1,17},{... | collective-permute-start | bytes 442376 | tf_op jit(solution)/shard_map/ppermute | solution.py:35
  355.3 13.9 %collective-permute-start.14 = (bf16[104,2304]{1,0:T(8,128)(2,1)S(1)}, bf16[104,2304]{1,0:T(8,128)(2,1)S(1)}, u32[]{:S(2)}, u32[]{:S(2)}) collective-permute-start(bf16[104,2304]{1,0:T(8,128)(2,1)S(1)} %constant_dynamic-slice_fusion.8), channel_id=1, source_target_pairs={{0,4},{4,0},{8,12},{12,8},{16,20},{20,16},{24,28},{28,24},{1,5},{5... | collective-permute-start | bytes 1437704 | tf_op jit(solution)/shard_map/ppermute | solution.py:35
  357.1 8.4 %collective-permute-start.33 = (bf16[96,768]{1,0:T(8,128)(2,1)S(1)}, bf16[96,768]{1,0:T(8,128)(2,1)S(1)}, u32[]{:S(2)}, u32[]{:S(2)}) collective-permute-start(bf16[96,768]{1,0:T(8,128)(2,1)S(1)} %add_convert_fusion.10), channel_id=1, source_target_pairs={{0,16},{4,20},{8,24},{12,28},{16,0},{20,4},{24,8},{28,12},{1,17},{... | collective-permute-start | bytes 442376 | tf_op jit(solution)/shard_map/ppermute | solution.py:35
  359.8 25.2 %collective-permute-start.22 = (bf16[96,3840]{1,0:T(8,128)(2,1)S(1)}, bf16[96,3840]{1,0:T(8,128)(2,1)S(1)}, u32[]{:S(2)}, u32[]{:S(2)}) collective-permute-start(bf16[96,3840]{1,0:T(8,128)(2,1)S(1)} %constant_dynamic-slice_fusion.5), channel_id=1, source_target_pairs={{0,4},{4,0},{8,12},{12,8},{16,20},{20,16},{24,28},{28,24},{1,5},{5... | collective-permute-start | bytes 2211848 | tf_op jit(solution)/shard_map/ppermute | solution.py:35
  365.6 9.9 %collective-permute-start.34 = (bf16[192,768]{1,0:T(8,128)(2,1)S(1)}, bf16[192,768]{1,0:T(8,128)(2,1)S(1)}, u32[]{:S(2)}, u32[]{:S(2)}) collective-permute-start(bf16[192,768]{1,0:T(8,128)(2,1)S(1)} %maximum_select_fusion.14), channel_id=1, source_target_pairs={{0,8},{4,12},{8,0},{12,4},{16,24},{20,28},{24,16},{28,20},{1,9},{5... | collective-permute-start | bytes 884744 | tf_op jit(solution)/shard_map/ppermute | solution.py:35
  369.4 15.8 %collective-permute-start.15 = (bf16[52,2304]{1,0:T(8,128)(2,1)S(1)}, bf16[52,2304]{1,0:T(8,128)(2,1)S(1)}, u32[]{:S(2)}, u32[]{:S(2)}) collective-permute-start(bf16[52,2304]{1,0:T(8,128)(2,1)S(1)} %constant_dynamic-slice_fusion.7), channel_id=1, source_target_pairs={{0,8},{4,12},{8,0},{12,4},{16,24},{20,28},{24,16},{28,20},{1,9},{5... | collective-permute-start | bytes 718856 | tf_op jit(solution)/shard_map/ppermute | solution.py:35
  375.7 41.2 %collective-permute-start.35 = (bf16[384,768]{1,0:T(8,128)(2,1)S(1)}, bf16[384,768]{1,0:T(8,128)(2,1)S(1)}, u32[]{:S(2)}, u32[]{:S(2)}) collective-permute-start(bf16[384,768]{1,0:T(8,128)(2,1)S(1)} %maximum_select_fusion.11), channel_id=1, source_target_pairs={{0,4},{4,0},{8,12},{12,8},{16,20},{20,16},{24,28},{28,24},{1,5},{5... | collective-permute-start | bytes 1769480 | tf_op jit(solution)/shard_map/ppermute | solution.py:35
  385.4 8.6 %collective-permute-start.16 = (bf16[26,2304]{1,0:T(8,128)(2,1)S(1)}, bf16[26,2304]{1,0:T(8,128)(2,1)S(1)}, u32[]{:S(2)}, u32[]{:S(2)}) collective-permute-start(bf16[26,2304]{1,0:T(8,128)(2,1)S(1)} %constant_dynamic-slice_fusion.6), channel_id=1, source_target_pairs={{0,16},{4,20},{8,24},{12,28},{16,0},{20,4},{24,8},{28,12},{1,17},{... | collective-permute-start | bytes 359432 | tf_op jit(solution)/shard_map/ppermute | solution.py:35
  388.3 10.8 %collective-permute-start.23 = (bf16[48,3840]{1,0:T(8,128)(2,1)S(1)}, bf16[48,3840]{1,0:T(8,128)(2,1)S(1)}, u32[]{:S(2)}, u32[]{:S(2)}) collective-permute-start(bf16[48,3840]{1,0:T(8,128)(2,1)S(1)} %constant_dynamic-slice_fusion.4), channel_id=1, source_target_pairs={{0,8},{4,12},{8,0},{12,4},{16,24},{20,28},{24,16},{28,20},{1,9},{5... | collective-permute-start | bytes 1105928 | tf_op jit(solution)/shard_map/ppermute | solution.py:35
  399.2 12.9 %collective-permute-start.24 = (bf16[24,3840]{1,0:T(8,128)(2,1)S(1)}, bf16[24,3840]{1,0:T(8,128)(2,1)S(1)}, u32[]{:S(2)}, u32[]{:S(2)}) collective-permute-start(bf16[24,3840]{1,0:T(8,128)(2,1)S(1)} %constant_dynamic-slice_fusion.3), channel_id=1, source_target_pairs={{0,16},{4,20},{8,24},{12,28},{16,0},{20,4},{24,8},{28,12},{1,17},{... | collective-permute-start | bytes 552968 | tf_op jit(solution)/shard_map/ppermute | solution.py:35
  401.9 10.3 %collective-permute-start.18 = (bf16[52,2304]{1,0:T(8,128)(2,1)S(1)}, bf16[52,2304]{1,0:T(8,128)(2,1)S(1)}, u32[]{:S(2)}, u32[]{:S(2)}) collective-permute-start(bf16[52,2304]{1,0:T(8,128)(2,1)S(1)} %maximum_select_fusion.15), channel_id=1, source_target_pairs={{0,8},{4,12},{8,0},{12,4},{16,24},{20,28},{24,16},{28,20},{1,9},{5... | collective-permute-start | bytes 718856 | tf_op jit(solution)/shard_map/ppermute | solution.py:35
  412.4 11.2 %collective-permute-start.19 = (bf16[104,2304]{1,0:T(8,128)(2,1)S(1)}, bf16[104,2304]{1,0:T(8,128)(2,1)S(1)}, u32[]{:S(2)}, u32[]{:S(2)}) collective-permute-start(bf16[104,2304]{1,0:T(8,128)(2,1)S(1)} %maximum_select_fusion.12), channel_id=1, source_target_pairs={{0,4},{4,0},{8,12},{12,8},{16,20},{20,16},{24,28},{28,24},{1,5},{5... | collective-permute-start | bytes 1437704 | tf_op jit(solution)/shard_map/ppermute | solution.py:35
  428.0 12.0 %collective-permute-start.27 = (bf16[96,3840]{1,0:T(8,128)(2,1)S(1)}, bf16[96,3840]{1,0:T(8,128)(2,1)S(1)}, u32[]{:S(2)}, u32[]{:S(2)}) collective-permute-start(bf16[96,3840]{1,0:T(8,128)(2,1)S(1)} %maximum_select_fusion.10), channel_id=1, source_target_pairs={{0,4},{4,0},{8,12},{12,8},{16,20},{20,16},{24,28},{28,24},{1,5},{5... | collective-permute-start | bytes 2211848 | tf_op jit(solution)/shard_map/ppermute | solution.py:35
  (53 other events, 566.2 us)
